TPU v7x, 32 devices: a whole 2x2x4 slice. The times are simulated.
32 devices in a mesh: doc: 8 (over z, core), clu: 4 (over y, x).
Axes of the slice: x: 2, y: 2, z: 4, core: 2. Of those that a mesh axis runs over, the one named last changes fastest.
Arguments:
- embeddings: bfloat16 [4096, 256], P(('doc', 'clu')), may hold values from -16 to 16
- centroids: bfloat16 [4096, 256], P('clu'), may hold values from -1 to 1
Outputs:
- new_centroids: float32 [256, 4096], P('doc', 'clu')
- cluster_mass: float32 [4096], P('clu')
All inputs are finite; a program needn't handle non-finite values.
Results may differ from a plain program's by a relative error of at most 0.0011.
Values may be sent and summed in bfloat16 or wider, within the bound.
A program may use at most 64 MiB of HBM per device.

v0:
```python
import functools
import math

import jax
import jax.numpy as jnp
from jax import lax
from jax.experimental import pallas as pl
from jax.experimental.pallas import tpu as pltpu
from jax.sharding import PartitionSpec as P

ITERS = 2
SMOOTHING = 0.05
LOG2E = math.log2(math.e)
MESH = pl.DeviceIdType.MESH
F32 = jnp.float32


def kernel(
    nd, nc,
    emb_ref, cent_ref, out_ref, mass_ref,
    emb_all, centers, scores, plan, rpot, colbuf, rowbuf, massbuf, sqbuf, sums, rsbuf, tot, pairbuf,
    own_sem, cent_sem, emb_ss, emb_rs, fwd_ss, col_ss, col_rs, row_ss, row_rs,
    mass_ss, mass_rs, sq_ss, sq_rs, sum_ss, sum_rs, pair_ss, pair_rs,
):
    nz = nd // 2
    nb = 2 * nc
    rows, features = emb_ref.shape
    half = cent_ref.shape[0] // 2
    own_f = features // nd
    log_docs = math.log2(rows * nd * nc)
    log_clusters = math.log2(2 * half * nc)
    d = lax.axis_index("doc")
    c = lax.axis_index("clu")
    core = lax.rem(d, 2)
    z = lax.div(d, 2)
    partner = d + 1 - 2 * core
    me = core * nc + c

    def block_peer(k):
        peer = lax.rem(me + k, nb)
        return peer, (2 * z + lax.div(peer, nc), lax.rem(peer, nc))

    def z_peer(k):
        peer = lax.rem(z + k, nz)
        return peer, (2 * peer + core, c)

    def doc_peer(k):
        peer = lax.rem(d + k, nd)
        return peer, (peer, c)

    def remote(src, dst, ss, rs, device):
        return pltpu.make_async_remote_copy(
            src_ref=src, dst_ref=dst, send_sem=ss, recv_sem=rs,
            device_id=device, device_id_type=MESH,
        )

    sends = []

    def send(*args):
        copy = remote(*args)
        copy.start()
        sends.append(copy)

    own_copy = pltpu.make_async_copy(emb_ref, emb_all.at[me], own_sem)
    own_copy.start()
    cent_copy = pltpu.make_async_copy(
        cent_ref.at[pl.ds(pl.multiple_of(core * half, half), half), :], centers, cent_sem
    )
    cent_copy.start()
    barrier = pltpu.get_barrier_semaphore()
    for k in range(1, nb):
        pl.semaphore_signal(barrier, inc=1, device_id=block_peer(k)[1], device_id_type=MESH)
    for k in range(1, nd):
        pl.semaphore_signal(barrier, inc=1, device_id=doc_peer(k)[1], device_id_type=MESH)

    def col_update(state, t):
        high, total = state
        t = t.reshape(rows // 8, 8, half)
        new = jnp.maximum(high, jnp.max(t, axis=0))
        total = total * jnp.exp2(high - new) + jnp.sum(jnp.exp2(t - new[None]), axis=0)
        return new, total

    state = (jnp.full((8, half), -jnp.inf, F32), jnp.zeros((8, half), F32))

    def first_block(state, slot):
        s = lax.dot_general(
            emb_all[slot], centers[...], (((1,), (1,)), ((), ())), preferred_element_type=F32
        ) * (LOG2E / SMOOTHING)
        scores[slot] = s
        return col_update(state, s)

    def arrive(slot):
        remote(
            emb_all.at[slot], emb_all.at[slot], emb_ss.at[0], emb_rs.at[slot], (partner, c)
        ).wait_recv()

    def clu_peer(k):
        if nc & (nc - 1):
            return lax.rem(c + k, nc)
        bits = [1 << i for i in range(nc.bit_length() - 1)]
        return sum(lax.rem(lax.div(c, b) + k // b, 2) * b for b in bits)

    own_copy.wait()
    cent_copy.wait()
    state = first_block(state, me)
    pl.semaphore_wait(barrier, nb - 1 + nd - 1)

    own = emb_all.at[me]
    for k in reversed(range(1, nc)):
        send(own, own, emb_ss.at[k], emb_rs.at[me], (d, clu_peer(k)))
    send(own, own, emb_ss.at[0], emb_rs.at[me], (partner, c))
    other = 1 - core
    for k in range(1, nc):
        slot = core * nc + clu_peer(k)
        arrive(slot)
        send(emb_all.at[slot], emb_all.at[slot], fwd_ss.at[k], emb_rs.at[slot], (partner, c))
        state = first_block(state, slot)
    for k in range(nc):
        slot = other * nc + clu_peer(k)
        arrive(slot)
        state = first_block(state, slot)

    diagonal = lax.broadcasted_iota(jnp.int32, (rows, rows), 0) == lax.broadcasted_iota(
        jnp.int32, (rows, rows), 1
    )

    def to_lanes(x):
        return jnp.sum(jnp.where(diagonal, x, 0.0), axis=0, keepdims=True)

    def to_sublanes(x):
        return jnp.sum(jnp.where(diagonal, x, 0.0), axis=1, keepdims=True)

    def column_potential(it, state):
        high, total = state
        top = jnp.max(high, axis=0, keepdims=True)
        total = jnp.sum(total * jnp.exp2(high - top), axis=0, keepdims=True)
        colbuf[it, z] = top + jnp.log2(total)
        mine = colbuf.at[it, z]
        for k in range(1, nz):
            send(mine, mine, col_ss.at[it, k], col_rs.at[it, z], z_peer(k)[1])
        for k in range(1, nz):
            peer, device = z_peer(k)
            theirs = colbuf.at[it, peer]
            remote(theirs, theirs, col_ss.at[it, k], col_rs.at[it, peer], device).wait_recv()
        logs = [colbuf[it, s] for s in range(nz)]
        top = functools.reduce(jnp.maximum, logs)
        return -log_clusters - (top + jnp.log2(sum(jnp.exp2(x - top) for x in logs)))

    part = nb // 2

    def row_send(it, h, col_pot):
        def block(b, carry):
            t = scores[h * part + b] + col_pot
            high = jnp.max(t, axis=1, keepdims=True)
            total = jnp.sum(jnp.exp2(t - high), axis=1, keepdims=True)
            rowbuf[it, h, me, pl.ds(b, 1), :] = to_lanes(high + jnp.log2(total))
            return carry

        lax.fori_loop(0, part, block, 0, unroll=4)
        mine = rowbuf.at[it, h, me]
        for k in range(1, nb):
            send(mine, mine, row_ss.at[it, h, k], row_rs.at[it, h, me], block_peer(k)[1])

    def row_receive(it, h):
        for k in range(1, nb):
            peer, device = block_peer(k)
            theirs = rowbuf.at[it, h, peer]
            remote(
                theirs, theirs, row_ss.at[it, h, k], row_rs.at[it, h, peer], device
            ).wait_recv()
        logs = rowbuf[it, h]
        top = jnp.max(logs, axis=0)
        total = jnp.sum(jnp.exp2(logs - top[None]), axis=0)
        rpot[h] = -log_docs - (top + jnp.log2(total))

    for it in range(ITERS):
        if it > 0:
            state = (jnp.full((8, half), -jnp.inf, F32), jnp.zeros((8, half), F32))
            for h in range(2):
                def again(b, state):
                    t = scores[h * part + b] + to_sublanes(rpot[h, pl.ds(b, 1), :])
                    return col_update(state, t)

                row_receive(it - 1, h)
                state = lax.fori_loop(0, part, again, state, unroll=4)
        col_pot = column_potential(it, state)
        for h in range(2):
            row_send(it, h, col_pot)

    mass = jnp.zeros((8, half), F32)
    for h in range(2):
        def plan_block(b, mass):
            t = scores[h * part + b] + to_sublanes(rpot[h, pl.ds(b, 1), :]) + col_pot + log_docs
            p = jnp.exp2(t)
            plan[h, pl.ds(pl.multiple_of(b * rows, rows), rows), :] = p.astype(jnp.bfloat16)
            return mass + jnp.sum(p.reshape(rows // 8, 8, half), axis=0)

        row_receive(ITERS - 1, h)
        mass = lax.fori_loop(0, part, plan_block, mass, unroll=4)
        product = lax.dot_general(
            emb_all[h * part:(h + 1) * part].reshape(part * rows, features), plan[h],
            (((0,), (0,)), ((), ())), preferred_element_type=F32,
        )
        sums[...] = product if h == 0 else sums[...] + product
    massbuf[d] = jnp.sum(mass, axis=0, keepdims=True)
    far = sorted(range(1, nz), key=lambda k: -min(k, nz - k))

    def share(peer):
        return sums.at[pl.ds(pl.multiple_of(peer * 2 * own_f, 2 * own_f), 2 * own_f), :]

    for k in far:
        peer, device = z_peer(k)
        send(share(peer), rsbuf.at[z], sum_ss.at[k], sum_rs.at[z], device)
    for k in range(1, nd):
        send(massbuf.at[d], massbuf.at[d], mass_ss.at[k], mass_rs.at[d], doc_peer(k)[1])
    total = share(z)[...]
    for k in reversed(far):
        peer, device = z_peer(k)
        remote(share(z), rsbuf.at[peer], sum_ss.at[k], sum_rs.at[peer], device).wait_recv()
        total = total + rsbuf[peer]
    tot[...] = total
    sqbuf[d] = jnp.sum(total * total, axis=0, keepdims=True)

    def features_of(which):
        return tot.at[pl.ds(pl.multiple_of(which * own_f, own_f), own_f), :]

    for k in range(1, nd):
        send(sqbuf.at[d], sqbuf.at[d], sq_ss.at[k], sq_rs.at[d], doc_peer(k)[1])
    send(features_of(other), pairbuf, pair_ss, pair_rs, (partner, c))
    for k in range(1, nd):
        peer, device = doc_peer(k)
        theirs = massbuf.at[peer]
        remote(theirs, theirs, mass_ss.at[k], mass_rs.at[peer], device).wait_recv()
        theirs = sqbuf.at[peer]
        remote(theirs, theirs, sq_ss.at[k], sq_rs.at[peer], device).wait_recv()
    remote(features_of(core), pairbuf, pair_ss, pair_rs, (partner, c)).wait_recv()

    def finish(which, block):
        columns = pl.ds(pl.multiple_of(which * half, half), half)
        squares = sum(sqbuf[2 * s + which] for s in range(nz))
        out_ref[:, columns] = block * lax.rsqrt(squares / features + 1e-06)
        mass_ref[:, columns] = sum(massbuf[2 * s + which] for s in range(nz)) * (
            2 * half * nc / (rows * nd * nc)
        )

    finish(core, features_of(core)[...])
    finish(other, pairbuf[...])
    for copy in sends:
        copy.wait_send()


def local(nd, nc, embeddings, centroids):
    rows, features = embeddings.shape
    own_cols = centroids.shape[0]
    half, nz, nb = own_cols // 2, nd // 2, 2 * nc
    own_f = features // nd
    dma = pltpu.SemaphoreType.DMA
    out, mass = pl.pallas_call(
        functools.partial(kernel, nd, nc),
        out_shape=(
            jax.ShapeDtypeStruct((own_f, own_cols), F32),
            jax.ShapeDtypeStruct((1, own_cols), F32),
        ),
        in_specs=[pl.BlockSpec(memory_space=pltpu.HBM)] * 2,
        out_specs=(pl.BlockSpec(memory_space=pltpu.VMEM),) * 2,
        scratch_shapes=[
            pltpu.VMEM((nb, rows, features), jnp.bfloat16),
            pltpu.VMEM((half, features), jnp.bfloat16),
            pltpu.VMEM((nb, rows, half), F32),
            pltpu.VMEM((2, nc * rows, half), jnp.bfloat16),
            pltpu.VMEM((2, nc, rows), F32),
            pltpu.VMEM((ITERS, nz, 1, half), F32),
            pltpu.VMEM((ITERS, 2, nb, nc, rows), F32),
            pltpu.VMEM((nd, 1, half), F32),
            pltpu.VMEM((nd, 1, half), F32),
            pltpu.VMEM((features, half), F32),
            pltpu.VMEM((nz, 2 * own_f, half), F32),
            pltpu.VMEM((2 * own_f, half), F32),
            pltpu.VMEM((own_f, half), F32),
            dma, dma, dma((nc,)), dma((nb,)), dma((nc,)),
            dma((ITERS, nz)), dma((ITERS, nz)), dma((ITERS, 2, nb)), dma((ITERS, 2, nb)),
            dma((nd,)), dma((nd,)), dma((nd,)), dma((nd,)),
            dma((nz,)), dma((nz,)), dma, dma,
        ],
        compiler_params=pltpu.CompilerParams(
            collective_id=0, has_side_effects=True
        ),
    )(embeddings, centroids)
    return out, mass.reshape(own_cols)


def solution(mesh):
    placed = (P(("doc", "clu"), None), P("clu", None))
    body = functools.partial(local, mesh.shape["doc"], mesh.shape["clu"])
    return jax.shard_map(
        body, mesh=mesh, in_specs=placed, out_specs=(P("doc", "clu"), P("clu")), check_vma=False
    )
```

profile of v0, /device:TPU:0, one launch (start us, length us, event | category | flops | bytes accessed | tf_op | source)
XLA Modules:
  0.0 49.2 jit_solution(13911728465356802334)
XLA Ops:
  0.6 46.3 %shard_map.41 = (f32[32,1024]{1,0:T(8,128)}, f32[1,1024]{1,0:T(1,128)}) custom-call(bf16[128,256]{1,0:T(8,128)(2,1)} %emb_ref.1, bf16[1024,256]{1,0:T(8,128)(2,1)} %cent_ref.1), custom_call_target="tpu_custom_call" | custom-call | tf_op jit(solution)/shard_map/pallas_call | solution.py:258
  47.0 0.0 copy-start
  47.0 1.6 %copy.6 = f32[32,1024]{1,0:T(8,128)} copy(f32[32,1024]{1,0:T(8,128)} %get-tuple-element.8) | data formatting | bytes 262144
  48.6 0.0 copy-done
  48.6 0.6 %copy.7 = f32[1024]{0:T(1024)} copy(f32[1024]{0:T(1024)S(1)} %bitcast.1) | data formatting | bytes 8192
Async XLA Ops:
  47.0 1.6 %copy-start = (f32[1,1024]{1,0:T(1,128)S(1)}, f32[1,1024]{1,0:T(1,128)}, u32[]{:S(2)}) copy-start(f32[1,1024]{1,0:T(1,128)} %get-tuple-element.5) | copy-start | bytes 12292
where the time goes:
time: 49.3 us; the launch traced here: 49.2 us
  Pallas kernels  46.3 us (94%)
  local copies, waits for them, and re-layouts  2.17 us (4%)
  between operations  0.65 us (1%)
    pallas_call x1, Pallas kernels, local(): pl.pallas_call(functools.partial(kernel, nd, nc), out_shape=(jax.ShapeDty...  46.3 us
    unnamed x4, local copies, waits for them, and re-layouts  2.17 us

commit v1 on v0

--- a/solution.py
+++ b/solution.py
@@ -15,7 +15,7 @@
 F32 = jnp.float32
 
 
-def kernel(
+def scattered_kernel(
     nd, nc,
     emb_ref, cent_ref, out_ref, mass_ref,
     emb_all, centers, scores, plan, rpot, colbuf, rowbuf, massbuf, sqbuf, sums, rsbuf, tot, pairbuf,
@@ -249,14 +249,14 @@
         copy.wait_send()
 
 
-def local(nd, nc, embeddings, centroids):
+def scattered(nd, nc, embeddings, centroids):
     rows, features = embeddings.shape
     own_cols = centroids.shape[0]
     half, nz, nb = own_cols // 2, nd // 2, 2 * nc
     own_f = features // nd
     dma = pltpu.SemaphoreType.DMA
     out, mass = pl.pallas_call(
-        functools.partial(kernel, nd, nc),
+        functools.partial(scattered_kernel, nd, nc),
         out_shape=(
             jax.ShapeDtypeStruct((own_f, own_cols), F32),
             jax.ShapeDtypeStruct((1, own_cols), F32),
@@ -289,6 +289,385 @@
     return out, mass.reshape(own_cols)
 
 
+def replicated_kernel(
+    nd, nc,
+    emb_ref, cent_ref, out_ref, mass_ref,
+    emb_all, centers, scores, plan, high, total, wide, rpot, zpot, colbuf, rowbuf, sums, finished, pairbuf, pairmass,
+    own_sem, cent_sem, own_ss, emb_rs, core_ss, plane_ss, col_ss, col_rs, row_ss, row_rs,
+    zp_ss, zp_rs, pair_ss, pair_rs,
+):
+    nz = nd // 2
+    nb = 2 * nc
+    rows, features = emb_ref.shape
+    half = cent_ref.shape[0] // 2
+    own_f = features // nd
+    docs, clusters = rows * nd * nc, 2 * half * nc
+    log_docs, log_clusters = math.log2(docs), math.log2(clusters)
+    d = lax.axis_index("doc")
+    c = lax.axis_index("clu")
+    core = lax.rem(d, 2)
+    other = 1 - core
+    z = lax.div(d, 2)
+    partner = d + other - core
+    me = core * nc + c
+    step = min(half, 64)
+    tiles = step // 8
+
+    def paired(i, k, n):
+        if n & (n - 1):
+            return lax.rem(i + k, n)
+        bits = [1 << b for b in range(n.bit_length() - 1)]
+        return sum(lax.rem(lax.div(i, b) + k // b, 2) * b for b in bits)
+
+    def block_peer(k):
+        peer = paired(me, k, nb)
+        return peer, (2 * z + lax.div(peer, nc), lax.rem(peer, nc))
+
+    def clu_peer(k):
+        return paired(c, k, nc)
+
+    def z_peer(k):
+        return paired(z, k, nz)
+
+    def slot_of(plane, side, cluster):
+        return plane * nb + side * nc + cluster
+
+    def remote(src, dst, ss, rs, device):
+        return pltpu.make_async_remote_copy(
+            src_ref=src, dst_ref=dst, send_sem=ss, recv_sem=rs,
+            device_id=device, device_id_type=MESH,
+        )
+
+    sends = []
+
+    def send(*args):
+        copy = remote(*args)
+        copy.start()
+        sends.append(copy)
+
+    mine = slot_of(z, core, c)
+    own = emb_all.at[mine]
+    own_copy = pltpu.make_async_copy(emb_ref, own, own_sem)
+    own_copy.start()
+    cent_copy = pltpu.make_async_copy(
+        cent_ref.at[pl.ds(pl.multiple_of(core * half, half), half), :], centers, cent_sem
+    )
+    cent_copy.start()
+    barrier = pltpu.get_barrier_semaphore()
+    for k in range(1, nb):
+        pl.semaphore_signal(barrier, inc=1, device_id=block_peer(k)[1], device_id_type=MESH)
+    for k in range(1, nz):
+        pl.semaphore_signal(
+            barrier, inc=1, device_id=(2 * z_peer(k) + core, c), device_id_type=MESH
+        )
+
+    def score(slot):
+        return lax.dot_general(
+            centers[...], emb_all[slot], (((1,), (1,)), ((), ())), preferred_element_type=F32
+        ) * (LOG2E / SMOOTHING)
+
+    def arrive(slot):
+        remote(
+            emb_all.at[slot], emb_all.at[slot], own_ss.at[0], emb_rs.at[slot], (partner, c)
+        ).wait_recv()
+
+    def to_partner(slot, k):
+        send(emb_all.at[slot], emb_all.at[slot], core_ss.at[k], emb_rs.at[slot], (partner, c))
+
+    def to_plane(slot, k):
+        for j in reversed(range(1, nc)):
+            send(
+                emb_all.at[slot], emb_all.at[slot], plane_ss.at[k, j], emb_rs.at[slot],
+                (d, clu_peer(j)),
+            )
+
+    def plane_scores(k):
+        def body(b, carry):
+            slot = z_peer(k) * nb + b
+            scores[slot] = score(slot) + wide[...]
+            return carry
+
+        for j in range(nc):
+            arrive(slot_of(z_peer(k), other, clu_peer(j)))
+        lax.fori_loop(0, nb, body, 0, unroll=2)
+
+    def piece(g):
+        return pl.ds(pl.multiple_of(g * step, step), step)
+
+    def column_update(slots, first):
+        def body(g, carry):
+            at = piece(g)
+            ts = [scores[s, at, :] for s in slots]
+            old = None if first else high[at, :]
+            new = functools.reduce(jnp.maximum, ts if first else ts + [old])
+            part = sum(jnp.exp2(t - new) for t in ts)
+            total[at, :] = part if first else part + total[at, :] * jnp.exp2(old - new)
+            high[at, :] = new
+            return carry
+
+        lax.fori_loop(0, half // step, body, 0, unroll=2)
+
+    own_copy.wait()
+    cent_copy.wait()
+    scores[mine] = score(mine)
+    pl.semaphore_wait(barrier, nb - 1 + nz - 1)
+
+    to_plane(mine, 0)
+    to_partner(mine, 0)
+    for k in range(1, nz):
+        send(own, own, own_ss.at[k], emb_rs.at[mine], (2 * z_peer(k) + core, c))
+    column_update([mine], True)
+    for k in range(1, nc):
+        slot = slot_of(z, core, clu_peer(k))
+        arrive(slot)
+        to_partner(slot, k)
+        scores[slot] = score(slot)
+    column_update([slot_of(z, core, clu_peer(k)) for k in range(1, nc)], False)
+
+    def from_plane(k):
+        slot = slot_of(z_peer(k), core, c)
+        arrive(slot)
+        to_plane(slot, k)
+        to_partner(slot, k * nc)
+
+    def across(k):
+        for j in range(1, nc):
+            slot = slot_of(z_peer(k), core, clu_peer(j))
+            arrive(slot)
+            to_partner(slot, k * nc + j)
+
+    early = list(range(1, nz))[:-1]
+    late = list(range(1, nz))[-1:]
+    for k in early[:1]:
+        from_plane(k)
+    for k in range(nc):
+        slot = slot_of(z, other, clu_peer(k))
+        arrive(slot)
+        scores[slot] = score(slot)
+        if k % 2:
+            column_update([slot_of(z, other, clu_peer(k - 1)), slot], False)
+    if nc % 2:
+        column_update([slot_of(z, other, clu_peer(nc - 1))], False)
+
+    def spread(x):
+        wide[...] = jnp.transpose(jnp.broadcast_to(x, (rows, half)))
+
+    def column_send(it, x):
+        colbuf[it, z] = x
+        ref = colbuf.at[it, z]
+        for k in range(1, nz):
+            send(ref, ref, col_ss.at[it, k], col_rs.at[it, z], (2 * z_peer(k) + core, c))
+
+    def column_receive(it):
+        for k in range(1, nz):
+            theirs = colbuf.at[it, z_peer(k)]
+            remote(
+                theirs, theirs, col_ss.at[it, k], col_rs.at[it, z_peer(k)], (partner, c)
+            ).wait_recv()
+        return [colbuf[it, s] for s in range(nz)]
+
+    def row_send(it):
+        ref = rowbuf.at[it, me]
+        for k in range(1, nb):
+            send(ref, ref, row_ss.at[it, k], row_rs.at[it, me], block_peer(k)[1])
+
+    def row_receive(it):
+        for k in range(1, nb):
+            peer, device = block_peer(k)
+            theirs = rowbuf.at[it, peer]
+            remote(theirs, theirs, row_ss.at[it, k], row_rs.at[it, peer], device).wait_recv()
+        return [rowbuf[it, s] for s in range(nb)]
+
+    def folded(x, op):
+        return functools.reduce(op, [x[8 * i:8 * i + 8] for i in range(tiles)])
+
+    def row_first(b, carry):
+        slot = z * nb + b
+        top = jnp.full((8, rows), -jnp.inf, F32)
+        for g in range(half // step):
+            at = pl.ds(g * step, step)
+            t = scores[slot, at, :] + wide[at, :]
+            scores[slot, at, :] = t
+            top = jnp.maximum(top, folded(t, jnp.maximum))
+        top = jnp.max(top, axis=0, keepdims=True)
+        acc = jnp.zeros((8, rows), F32)
+        for g in range(half // step):
+            at = pl.ds(g * step, step)
+            acc = acc + folded(jnp.exp2(scores[slot, at, :] - top), jnp.add)
+        rowbuf[0, me, pl.ds(b, 1), :] = top + jnp.log2(jnp.sum(acc, axis=0, keepdims=True))
+        return carry
+
+    def row_next(it, b, carry):
+        slot = z * nb + b
+        r = rpot[pl.ds(b, 1), :]
+        acc = jnp.zeros((8, rows), F32)
+        for g in range(half // step):
+            at = pl.ds(g * step, step)
+            t = scores[slot, at, :] + wide[at, :]
+            scores[slot, at, :] = t
+            acc = acc + folded(jnp.exp2(t + r), jnp.add)
+        rowbuf[it, me, pl.ds(b, 1), :] = jnp.sum(acc, axis=0, keepdims=True)
+        return carry
+
+    def column_next(g, carry):
+        at = piece(g)
+        acc = jnp.zeros((step, rows), F32)
+        for b in range(nb):
+            acc = acc + jnp.exp2(scores[z * nb + b, at, :] + rpot[pl.ds(b, 1), :])
+        total[at, :] = acc
+        return carry
+
+    tops = jnp.transpose(high[...])
+    top = jnp.max(tops, axis=0, keepdims=True)
+    column_send(
+        0,
+        top + jnp.log2(
+            jnp.sum(jnp.transpose(total[...]) * jnp.exp2(tops - top), axis=0, keepdims=True)
+        ),
+    )
+    for k in early[1:]:
+        from_plane(k)
+    logs = column_receive(0)
+    top = functools.reduce(jnp.maximum, logs)
+    col_pot = -log_clusters - (top + jnp.log2(sum(jnp.exp2(x - top) for x in logs)))
+    spread(col_pot)
+    lax.fori_loop(0, nb, row_first, 0, unroll=2)
+    row_send(0)
+    for k in early:
+        across(k)
+    logs = row_receive(0)
+    top = functools.reduce(jnp.maximum, logs)
+    rpot[...] = -log_docs - (top + jnp.log2(sum(jnp.exp2(x - top) for x in logs)))
+
+    for it in range(1, ITERS):
+        lax.fori_loop(0, half // step, column_next, 0, unroll=2)
+        column_send(it, jnp.sum(jnp.transpose(total[...]), axis=0, keepdims=True))
+        if it == 1:
+            for k in late:
+                from_plane(k)
+        change = -log_clusters - jnp.log2(sum(column_receive(it)))
+        col_pot = col_pot + change
+        spread(change)
+        lax.fori_loop(0, nb, functools.partial(row_next, it), 0, unroll=2)
+        row_send(it)
+        if it == 1:
+            for k in late:
+                across(k)
+        if it == ITERS - 1:
+            spread(col_pot)
+        for k in early if it == ITERS - 1 else ():
+            plane_scores(k)
+        rpot[...] = rpot[...] - log_docs - jnp.log2(sum(row_receive(it)))
+
+    zpot[z] = rpot[...] + log_docs
+    ref = zpot.at[z]
+    for k in range(1, nz):
+        send(ref, ref, zp_ss.at[k], zp_rs.at[z], (2 * z_peer(k) + core, c))
+
+    def plane_plan(plane, first):
+        def body(g, carry):
+            at = piece(g)
+            acc = jnp.zeros((step, rows), F32)
+            for b in range(nb):
+                p = jnp.exp2(scores[plane * nb + b, at, :] + zpot[plane, pl.ds(b, 1), :])
+                plan[at, b * rows:(b + 1) * rows] = p.astype(jnp.bfloat16)
+                acc = acc + p
+            total[at, :] = acc if first else acc + total[at, :]
+            return carry
+
+        lax.fori_loop(0, half // step, body, 0, unroll=2)
+        product = lax.dot_general(
+            plan[...], emb_all[pl.ds(plane * nb, nb)].reshape(nb * rows, features),
+            (((1,), (0,)), ((), ())), preferred_element_type=F32,
+        )
+        sums[...] = product if first else sums[...] + product
+
+    plane_plan(z, True)
+    for k in late:
+        plane_scores(k)
+    for k in range(1, nz):
+        plane = z_peer(k)
+        theirs = zpot.at[plane]
+        remote(theirs, theirs, zp_ss.at[k], zp_rs.at[plane], (partner, c)).wait_recv()
+        plane_plan(plane, False)
+
+    everything = jnp.transpose(sums[...])
+    scale = lax.rsqrt(jnp.sum(everything * everything, axis=0, keepdims=True) / features + 1e-06)
+    finished[...] = everything * scale
+    pairmass[0] = jnp.sum(jnp.transpose(total[...]), axis=0, keepdims=True) * (clusters / docs)
+
+    def features_of(which):
+        return finished.at[pl.ds(pl.multiple_of((2 * z + which) * own_f, own_f), own_f), :]
+
+    send(features_of(other), pairbuf, pair_ss.at[0], pair_rs.at[0], (partner, c))
+    send(pairmass.at[0], pairmass.at[1], pair_ss.at[1], pair_rs.at[1], (partner, c))
+    columns = pl.ds(pl.multiple_of(core * half, half), half)
+    out_ref[:, columns] = features_of(core)[...]
+    mass_ref[:, columns] = pairmass[0]
+    columns = pl.ds(pl.multiple_of(other * half, half), half)
+    remote(pairbuf, pairbuf, pair_ss.at[0], pair_rs.at[0], (partner, c)).wait_recv()
+    out_ref[:, columns] = pairbuf[...]
+    remote(
+        pairmass.at[1], pairmass.at[1], pair_ss.at[1], pair_rs.at[1], (partner, c)
+    ).wait_recv()
+    mass_ref[:, columns] = pairmass[1]
+    for copy in sends:
+        copy.wait_send()
+
+
+def replicated(nd, nc, embeddings, centroids):
+    rows, features = embeddings.shape
+    own_cols = centroids.shape[0]
+    half, nz, nb = own_cols // 2, nd // 2, 2 * nc
+    own_f = features // nd
+    dma = pltpu.SemaphoreType.DMA
+    out, mass = pl.pallas_call(
+        functools.partial(replicated_kernel, nd, nc),
+        out_shape=(
+            jax.ShapeDtypeStruct((own_f, own_cols), F32),
+            jax.ShapeDtypeStruct((1, own_cols), F32),
+        ),
+        in_specs=[pl.BlockSpec(memory_space=pltpu.HBM)] * 2,
+        out_specs=(pl.BlockSpec(memory_space=pltpu.VMEM),) * 2,
+        scratch_shapes=[
+            pltpu.VMEM((nz * nb, rows, features), jnp.bfloat16),
+            pltpu.VMEM((half, features), jnp.bfloat16),
+            pltpu.VMEM((nz * nb, half, rows), F32),
+            pltpu.VMEM((half, nb * rows), jnp.bfloat16),
+            pltpu.VMEM((half, rows), F32),
+            pltpu.VMEM((half, rows), F32),
+            pltpu.VMEM((half, rows), F32),
+            pltpu.VMEM((nb, rows), F32),
+            pltpu.VMEM((nz, nb, rows), F32),
+            pltpu.VMEM((ITERS, nz, 1, half), F32),
+            pltpu.VMEM((ITERS, nb, nb, rows), F32),
+            pltpu.VMEM((half, features), F32),
+            pltpu.VMEM((features, half), F32),
+            pltpu.VMEM((own_f, half), F32),
+            pltpu.VMEM((2, 1, half), F32),
+            dma, dma, dma((nz,)), dma((nz * nb,)), dma((nz * nc,)), dma((nz, nc)),
+            dma((ITERS, nz)), dma((ITERS, nz)), dma((ITERS, nb)), dma((ITERS, nb)),
+            dma((nz,)), dma((nz,)), dma((2,)), dma((2,)),
+        ],
+        compiler_params=pltpu.CompilerParams(
+            collective_id=0, has_side_effects=True, vmem_limit_bytes=VMEM_BYTES
+        ),
+    )(embeddings, centroids)
+    return out, mass.reshape(own_cols)
+
+
+VMEM_BYTES = 48 << 20
+
+
+def local(nd, nc, embeddings, centroids):
+    rows, features = embeddings.shape
+    docs = rows * nd * nc
+    half = centroids.shape[0] // 2
+    held = docs * (2 * features + 4 * half)
+    form = replicated if 2 * held <= VMEM_BYTES else scattered
+    return form(nd, nc, embeddings, centroids)
+
+
 def solution(mesh):
     placed = (P(("doc", "clu"), None), P("clu", None))
     body = functools.partial(local, mesh.shape["doc"], mesh.shape["clu"])

time: 49.3 us -> 39.6 us (0.80)
  Pallas kernels: 46.3 us -> 35.6 us
  local copies, waits for them, and re-layouts: 2.17 us -> 3.12 us
    pallas_call x1, Pallas kernels: 46.3 us -> 35.6 us  [replicated(): pl.pallas_call(functools.partial(replicated_kernel, nd, nc), out_shape=(j...]
    unnamed x4 -> x6, local copies, waits for them, and re-layouts: 2.17 us -> 3.12 us
where the time goes in v1:
time: 39.6 us; the launch traced here: 39.4 us
  Pallas kernels  35.6 us (90%)
  local copies, waits for them, and re-layouts  3.12 us (8%)
  between operations  0.65 us (2%)
    pallas_call x1, Pallas kernels, replicated(): pl.pallas_call(functools.partial(replicated_kernel, nd, nc), out_shape=(j...  35.6 us
    unnamed x6, local copies, waits for them, and re-layouts  3.12 us

profile of v1, /device:TPU:0, one launch (start us, length us, event | category | flops | bytes accessed | tf_op | source)
XLA Modules:
  0.0 39.4 jit_solution(8702810081486560224)
XLA Ops:
  0.6 0.0 copy-start
  0.6 1.0 %copy-done = bf16[1024,256]{1,0:T(8,128)(2,1)S(1)} copy-done((bf16[1024,256]{1,0:T(8,128)(2,1)S(1)}, bf16[1024,256]{1,0:T(8,128)(2,1)}, u32[]{:S(2)}) %copy-start) | copy-done | bytes 524312
  1.7 0.0 copy-start.1
  1.7 0.8 %copy-done.1 = bf16[128,256]{1,0:T(8,128)(2,1)S(1)} copy-done((bf16[128,256]{1,0:T(8,128)(2,1)S(1)}, bf16[128,256]{1,0:T(8,128)(2,1)}, u32[]{:S(2)}) %copy-start.1) | copy-done | bytes 65560
  2.5 35.6 %shard_map.41 = (f32[32,1024]{1,0:T(8,128)S(1)}, f32[1,1024]{1,0:T(1,128)S(1)}) custom-call(bf16[128,256]{1,0:T(8,128)(2,1)S(1)} %copy-done.1, bf16[1024,256]{1,0:T(8,128)(2,1)S(1)} %copy-done), custom_call_target="tpu_custom_call" | custom-call | tf_op jit(solution)/shard_map/pallas_call | solution.py:624
  38.1 0.7 %copy.6 = f32[32,1024]{1,0:T(8,128)} copy(f32[32,1024]{1,0:T(8,128)S(1)} %get-tuple-element.8) | data formatting | bytes 262144
  38.8 0.6 %copy.7 = f32[1024]{0:T(1024)} copy(f32[1024]{0:T(1024)S(1)} %bitcast.1) | data formatting | bytes 8192
Async XLA Ops:
  0.6 1.0 %copy-start = (bf16[1024,256]{1,0:T(8,128)(2,1)S(1)}, bf16[1024,256]{1,0:T(8,128)(2,1)}, u32[]{:S(2)}) copy-start(bf16[1024,256]{1,0:T(8,128)(2,1)} %cent_ref.1) | copy-start | bytes 1572868
  1.7 0.8 %copy-start.1 = (bf16[128,256]{1,0:T(8,128)(2,1)S(1)}, bf16[128,256]{1,0:T(8,128)(2,1)}, u32[]{:S(2)}) copy-start(bf16[128,256]{1,0:T(8,128)(2,1)} %emb_ref.1) | copy-start | bytes 196612

commit v2 on v1

--- a/solution.py
+++ b/solution.py
@@ -383,13 +383,18 @@
 
     def plane_scores(k):
         def body(b, carry):
-            slot = z_peer(k) * nb + b
-            scores[slot] = score(slot) + wide[...]
+            slot = z_peer(k) * nb + 2 * b
+            both = lax.dot_general(
+                centers[...], emb_all[pl.ds(slot, 2)].reshape(2 * rows, features),
+                (((1,), (1,)), ((), ())), preferred_element_type=F32,
+            ) * (LOG2E / SMOOTHING)
+            scores[slot] = both[:, :rows] + wide[...]
+            scores[slot + 1] = both[:, rows:] + wide[...]
             return carry
 
         for j in range(nc):
             arrive(slot_of(z_peer(k), other, clu_peer(j)))
-        lax.fori_loop(0, nb, body, 0, unroll=2)
+        lax.fori_loop(0, nb // 2, body, 0, unroll=2)
 
     def piece(g):
         return pl.ds(pl.multiple_of(g * step, step), step)
@@ -531,7 +536,7 @@
     top = functools.reduce(jnp.maximum, logs)
     col_pot = -log_clusters - (top + jnp.log2(sum(jnp.exp2(x - top) for x in logs)))
     spread(col_pot)
-    lax.fori_loop(0, nb, row_first, 0, unroll=2)
+    lax.fori_loop(0, nb, row_first, 0, unroll=4)
     row_send(0)
     for k in early:
         across(k)
@@ -540,7 +545,7 @@
     rpot[...] = -log_docs - (top + jnp.log2(sum(jnp.exp2(x - top) for x in logs)))
 
     for it in range(1, ITERS):
-        lax.fori_loop(0, half // step, column_next, 0, unroll=2)
+        lax.fori_loop(0, half // step, column_next, 0, unroll=4)
         column_send(it, jnp.sum(jnp.transpose(total[...]), axis=0, keepdims=True))
         if it == 1:
             for k in late:
@@ -548,7 +553,7 @@
         change = -log_clusters - jnp.log2(sum(column_receive(it)))
         col_pot = col_pot + change
         spread(change)
-        lax.fori_loop(0, nb, functools.partial(row_next, it), 0, unroll=2)
+        lax.fori_loop(0, nb, functools.partial(row_next, it), 0, unroll=4)
         row_send(it)
         if it == 1:
             for k in late:
@@ -575,7 +580,7 @@
             total[at, :] = acc if first else acc + total[at, :]
             return carry
 
-        lax.fori_loop(0, half // step, body, 0, unroll=2)
+        lax.fori_loop(0, half // step, body, 0, unroll=4)
         product = lax.dot_general(
             plan[...], emb_all[pl.ds(plane * nb, nb)].reshape(nb * rows, features),
             (((1,), (0,)), ((), ())), preferred_element_type=F32,
@@ -652,7 +657,7 @@
         compiler_params=pltpu.CompilerParams(
             collective_id=0, has_side_effects=True, vmem_limit_bytes=VMEM_BYTES
         ),
-    )(embeddings, centroids)
+    )(*(pltpu.with_memory_space_constraint(a, pltpu.HBM) for a in (embeddings, centroids)))
     return out, mass.reshape(own_cols)
 
 

time: 39.6 us -> 36.6 us (0.924)
  local copies, waits for them, and re-layouts: 3.12 us -> 1.25 us
  Pallas kernels: 35.6 us -> 34.5 us
    unnamed x6 -> x2, local copies, waits for them, and re-layouts: 3.12 us -> 1.25 us
    pallas_call x1, Pallas kernels: 35.6 us -> 34.5 us  [replicated(): pl.pallas_call(functools.partial(replicated_kernel, nd, nc), out_shape=(j...]
where the time goes in v2:
time: 36.6 us; the launch traced here: 36.4 us
  Pallas kernels  34.5 us (94%)
  local copies, waits for them, and re-layouts  1.25 us (3%)
  between operations  0.64 us (2%)
    pallas_call x1, Pallas kernels, replicated(): pl.pallas_call(functools.partial(replicated_kernel, nd, nc), out_shape=(j...  34.5 us
    unnamed x2, local copies, waits for them, and re-layouts  1.25 us

profile of v2, /device:TPU:0, one launch (start us, length us, event | category | flops | bytes accessed | tf_op | source)
XLA Modules:
  0.0 36.4 jit_solution(2047172194211936885)
XLA Ops:
  0.6 34.5 %shard_map.41 = (f32[32,1024]{1,0:T(8,128)S(1)}, f32[1,1024]{1,0:T(1,128)S(1)}) custom-call(bf16[128,256]{1,0:T(8,128)(2,1)} %emb_ref.1, bf16[1024,256]{1,0:T(8,128)(2,1)} %cent_ref.1), custom_call_target="tpu_custom_call" | custom-call | tf_op jit(solution)/shard_map/pallas_call | solution.py:629
  35.2 0.7 %copy.6 = f32[32,1024]{1,0:T(8,128)} copy(f32[32,1024]{1,0:T(8,128)S(1)} %get-tuple-element.8) | data formatting | bytes 262144
  35.8 0.6 %copy.7 = f32[1024]{0:T(1024)} copy(f32[1024]{0:T(1024)S(1)} %bitcast.1) | data formatting | bytes 8192

commit v3 on v2

--- a/solution.py
+++ b/solution.py
@@ -292,9 +292,9 @@
 def replicated_kernel(
     nd, nc,
     emb_ref, cent_ref, out_ref, mass_ref,
-    emb_all, centers, scores, plan, high, total, wide, rpot, zpot, colbuf, rowbuf, sums, finished, pairbuf, pairmass,
+    emb_all, centers, scores, plan, high, total, wide, pots, share, colbuf, rowbuf, sums, finished, pairbuf, pairmass,
     own_sem, cent_sem, own_ss, emb_rs, core_ss, plane_ss, col_ss, col_rs, row_ss, row_rs,
-    zp_ss, zp_rs, pair_ss, pair_rs,
+    pot_ss, pot_rs, pair_ss, pair_rs,
 ):
     nz = nd // 2
     nb = 2 * nc
@@ -374,27 +374,31 @@
     def to_partner(slot, k):
         send(emb_all.at[slot], emb_all.at[slot], core_ss.at[k], emb_rs.at[slot], (partner, c))
 
-    def to_plane(slot, k):
-        for j in reversed(range(1, nc)):
+    near = [j for j in range(1, nc) if not j & (j - 1)]
+    far = [j for j in range(1, nc) if j & (j - 1)]
+
+    def to_plane(slot, k, which):
+        for j in which:
             send(
                 emb_all.at[slot], emb_all.at[slot], plane_ss.at[k, j], emb_rs.at[slot],
                 (d, clu_peer(j)),
             )
 
-    def plane_scores(k):
-        def body(b, carry):
-            slot = z_peer(k) * nb + 2 * b
-            both = lax.dot_general(
-                centers[...], emb_all[pl.ds(slot, 2)].reshape(2 * rows, features),
-                (((1,), (1,)), ((), ())), preferred_element_type=F32,
-            ) * (LOG2E / SMOOTHING)
-            scores[slot] = both[:, :rows] + wide[...]
-            scores[slot + 1] = both[:, rows:] + wide[...]
-            return carry
-
-        for j in range(nc):
+    def pair_scores(k, side, pair):
+        slot = slot_of(z_peer(k), side, 2 * pair)
+        both = lax.dot_general(
+            centers[...], emb_all[pl.ds(slot, 2)].reshape(2 * rows, features),
+            (((1,), (1,)), ((), ())), preferred_element_type=F32,
+        ) * (LOG2E / SMOOTHING)
+        scores[slot] = both[:, :rows] + wide[...]
+        scores[slot + 1] = both[:, rows:] + wide[...]
+
+    def plane_scores(k, first, count):
+        for j in range(2 * first, 2 * (first + count)):
             arrive(slot_of(z_peer(k), other, clu_peer(j)))
-        lax.fori_loop(0, nb // 2, body, 0, unroll=2)
+        for j in range(first, first + count):
+            for side in (core, other):
+                pair_scores(k, side, paired(lax.div(c, 2), j, nc // 2))
 
     def piece(g):
         return pl.ds(pl.multiple_of(g * step, step), step)
@@ -417,7 +421,7 @@
     scores[mine] = score(mine)
     pl.semaphore_wait(barrier, nb - 1 + nz - 1)
 
-    to_plane(mine, 0)
+    to_plane(mine, 0, far + near)
     to_partner(mine, 0)
     for k in range(1, nz):
         send(own, own, own_ss.at[k], emb_rs.at[mine], (2 * z_peer(k) + core, c))
@@ -432,19 +436,17 @@
     def from_plane(k):
         slot = slot_of(z_peer(k), core, c)
         arrive(slot)
-        to_plane(slot, k)
+        to_plane(slot, k, near)
         to_partner(slot, k * nc)
 
-    def across(k):
-        for j in range(1, nc):
+    def across(k, which):
+        for j in which:
             slot = slot_of(z_peer(k), core, clu_peer(j))
             arrive(slot)
             to_partner(slot, k * nc + j)
 
-    early = list(range(1, nz))[:-1]
-    late = list(range(1, nz))[-1:]
-    for k in early[:1]:
-        from_plane(k)
+    if nz > 1:
+        from_plane(1)
     for k in range(nc):
         slot = slot_of(z, other, clu_peer(k))
         arrive(slot)
@@ -471,17 +473,19 @@
             ).wait_recv()
         return [colbuf[it, s] for s in range(nz)]
 
-    def row_send(it):
-        ref = rowbuf.at[it, me]
-        for k in range(1, nb):
-            send(ref, ref, row_ss.at[it, k], row_rs.at[it, me], block_peer(k)[1])
-
-    def row_receive(it):
-        for k in range(1, nb):
-            peer, device = block_peer(k)
-            theirs = rowbuf.at[it, peer]
-            remote(theirs, theirs, row_ss.at[it, k], row_rs.at[it, peer], device).wait_recv()
-        return [rowbuf[it, s] for s in range(nb)]
+    def row_send(it, k):
+        ref = rowbuf.at[it, k, me]
+        for j in range(1, nb):
+            send(ref, ref, row_ss.at[it, k, j], row_rs.at[it, k, me], block_peer(j)[1])
+
+    def row_receive(it, k):
+        for j in range(1, nb):
+            peer, device = block_peer(j)
+            theirs = rowbuf.at[it, k, peer]
+            remote(
+                theirs, theirs, row_ss.at[it, k, j], row_rs.at[it, k, peer], device
+            ).wait_recv()
+        return [rowbuf[it, k, s] for s in range(nb)]
 
     def folded(x, op):
         return functools.reduce(op, [x[8 * i:8 * i + 8] for i in range(tiles)])
@@ -499,26 +503,28 @@
         for g in range(half // step):
             at = pl.ds(g * step, step)
             acc = acc + folded(jnp.exp2(scores[slot, at, :] - top), jnp.add)
-        rowbuf[0, me, pl.ds(b, 1), :] = top + jnp.log2(jnp.sum(acc, axis=0, keepdims=True))
+        rowbuf[0, 0, me, pl.ds(b, 1), :] = top + jnp.log2(jnp.sum(acc, axis=0, keepdims=True))
         return carry
 
-    def row_next(it, b, carry):
-        slot = z * nb + b
-        r = rpot[pl.ds(b, 1), :]
+    def row_next(it, k, last, b, carry):
+        plane = z_peer(k)
+        slot = plane * nb + b
+        r = pots[plane, pl.ds(b, 1), :]
         acc = jnp.zeros((8, rows), F32)
         for g in range(half // step):
             at = pl.ds(g * step, step)
             t = scores[slot, at, :] + wide[at, :]
-            scores[slot, at, :] = t
-            acc = acc + folded(jnp.exp2(t + r), jnp.add)
-        rowbuf[it, me, pl.ds(b, 1), :] = jnp.sum(acc, axis=0, keepdims=True)
+            e = jnp.exp2(t + r)
+            scores[slot, at, :] = e if last else t
+            acc = acc + folded(e, jnp.add)
+        rowbuf[it, k, me, pl.ds(b, 1), :] = jnp.sum(acc, axis=0, keepdims=True)
         return carry
 
     def column_next(g, carry):
         at = piece(g)
         acc = jnp.zeros((step, rows), F32)
         for b in range(nb):
-            acc = acc + jnp.exp2(scores[z * nb + b, at, :] + rpot[pl.ds(b, 1), :])
+            acc = acc + jnp.exp2(scores[z * nb + b, at, :] + pots[z, pl.ds(b, 1), :])
         total[at, :] = acc
         return carry
 
@@ -530,71 +536,77 @@
             jnp.sum(jnp.transpose(total[...]) * jnp.exp2(tops - top), axis=0, keepdims=True)
         ),
     )
-    for k in early[1:]:
+    for k in range(1, nz):
+        for j in far:
+            slot = slot_of(z, core, clu_peer(j))
+            send(
+                emb_all.at[slot], emb_all.at[slot], plane_ss.at[k, j], emb_rs.at[slot],
+                (2 * z_peer(k) + core, c),
+            )
+    for k in range(2, nz):
         from_plane(k)
     logs = column_receive(0)
     top = functools.reduce(jnp.maximum, logs)
-    col_pot = -log_clusters - (top + jnp.log2(sum(jnp.exp2(x - top) for x in logs)))
-    spread(col_pot)
+    spread(-log_clusters - (top + jnp.log2(sum(jnp.exp2(x - top) for x in logs))))
     lax.fori_loop(0, nb, row_first, 0, unroll=4)
-    row_send(0)
-    for k in early:
-        across(k)
-    logs = row_receive(0)
+    row_send(0, 0)
+    for k in range(1, nz):
+        across(k, near + far if k == 1 else near)
+    for k in range(1, nz):
+        plane_scores(k, 0, nc // 2 if k == 1 else 1)
+    logs = row_receive(0, 0)
     top = functools.reduce(jnp.maximum, logs)
-    rpot[...] = -log_docs - (top + jnp.log2(sum(jnp.exp2(x - top) for x in logs)))
+    pots[z] = -log_docs - (top + jnp.log2(sum(jnp.exp2(x - top) for x in logs)))
 
     for it in range(1, ITERS):
+        last = it == ITERS - 1
+        if last:
+            ref = pots.at[z]
+            for k in range(1, nz):
+                send(ref, ref, pot_ss.at[k], pot_rs.at[z], (2 * z_peer(k) + core, c))
         lax.fori_loop(0, half // step, column_next, 0, unroll=4)
         column_send(it, jnp.sum(jnp.transpose(total[...]), axis=0, keepdims=True))
         if it == 1:
-            for k in late:
-                from_plane(k)
+            for k in range(2, nz):
+                across(k, far)
+            for k in range(2, nz):
+                plane_scores(k, 1, nc // 2 - 1)
         change = -log_clusters - jnp.log2(sum(column_receive(it)))
-        col_pot = col_pot + change
         spread(change)
-        lax.fori_loop(0, nb, functools.partial(row_next, it), 0, unroll=4)
-        row_send(it)
-        if it == 1:
-            for k in late:
-                across(k)
-        if it == ITERS - 1:
-            spread(col_pot)
-        for k in early if it == ITERS - 1 else ():
-            plane_scores(k)
-        rpot[...] = rpot[...] - log_docs - jnp.log2(sum(row_receive(it)))
-
-    zpot[z] = rpot[...] + log_docs
-    ref = zpot.at[z]
-    for k in range(1, nz):
-        send(ref, ref, zp_ss.at[k], zp_rs.at[z], (2 * z_peer(k) + core, c))
-
-    def plane_plan(plane, first):
-        def body(g, carry):
-            at = piece(g)
-            acc = jnp.zeros((step, rows), F32)
-            for b in range(nb):
-                p = jnp.exp2(scores[plane * nb + b, at, :] + zpot[plane, pl.ds(b, 1), :])
-                plan[at, b * rows:(b + 1) * rows] = p.astype(jnp.bfloat16)
-                acc = acc + p
-            total[at, :] = acc if first else acc + total[at, :]
-            return carry
-
-        lax.fori_loop(0, half // step, body, 0, unroll=4)
-        product = lax.dot_general(
-            plan[...], emb_all[pl.ds(plane * nb, nb)].reshape(nb * rows, features),
-            (((1,), (0,)), ((), ())), preferred_element_type=F32,
-        )
-        sums[...] = product if first else sums[...] + product
-
-    plane_plan(z, True)
-    for k in late:
-        plane_scores(k)
-    for k in range(1, nz):
+        for k in range(nz if last else 1):
+            if k:
+                theirs = pots.at[z_peer(k)]
+                remote(
+                    theirs, theirs, pot_ss.at[k], pot_rs.at[z_peer(k)], (partner, c)
+                ).wait_recv()
+            lax.fori_loop(0, nb, functools.partial(row_next, it, k, last), 0, unroll=4)
+            row_send(it, k)
+        if not last:
+            pots[z] = pots[z] - log_docs - jnp.log2(sum(row_receive(it, 0)))
+
+    wider = min(half, 256)
+
+    def plane_plan(k):
         plane = z_peer(k)
-        theirs = zpot.at[plane]
-        remote(theirs, theirs, zp_ss.at[k], zp_rs.at[plane], (partner, c)).wait_recv()
-        plane_plan(plane, False)
+        share[k] = 1.0 / sum(row_receive(ITERS - 1, k))
+        block = emb_all[pl.ds(plane * nb, nb)].reshape(nb * rows, features)
+        for g in range(half // wider):
+            for i in range(wider // step):
+                at = pl.ds(g * wider + i * step, step)
+                acc = jnp.zeros((step, rows), F32)
+                for b in range(nb):
+                    p = scores[plane * nb + b, at, :] * share[k, pl.ds(b, 1), :]
+                    plan[at, b * rows:(b + 1) * rows] = p.astype(jnp.bfloat16)
+                    acc = acc + p
+                total[at, :] = acc + total[at, :] if k else acc
+            at = pl.ds(g * wider, wider)
+            product = lax.dot_general(
+                plan[at, :], block, (((1,), (0,)), ((), ())), preferred_element_type=F32
+            )
+            sums[at, :] = sums[at, :] + product if k else product
+
+    for k in range(nz):
+        plane_plan(k)
 
     everything = jnp.transpose(sums[...])
     scale = lax.rsqrt(jnp.sum(everything * everything, axis=0, keepdims=True) / features + 1e-06)
@@ -642,16 +654,16 @@
             pltpu.VMEM((half, rows), F32),
             pltpu.VMEM((half, rows), F32),
             pltpu.VMEM((half, rows), F32),
-            pltpu.VMEM((nb, rows), F32),
+            pltpu.VMEM((nz, nb, rows), F32),
             pltpu.VMEM((nz, nb, rows), F32),
             pltpu.VMEM((ITERS, nz, 1, half), F32),
-            pltpu.VMEM((ITERS, nb, nb, rows), F32),
+            pltpu.VMEM((ITERS, nz, nb, nb, rows), F32),
             pltpu.VMEM((half, features), F32),
             pltpu.VMEM((features, half), F32),
             pltpu.VMEM((own_f, half), F32),
             pltpu.VMEM((2, 1, half), F32),
             dma, dma, dma((nz,)), dma((nz * nb,)), dma((nz * nc,)), dma((nz, nc)),
-            dma((ITERS, nz)), dma((ITERS, nz)), dma((ITERS, nb)), dma((ITERS, nb)),
+            dma((ITERS, nz)), dma((ITERS, nz)), dma((ITERS, nz, nb)), dma((ITERS, nz, nb)),
             dma((nz,)), dma((nz,)), dma((2,)), dma((2,)),
         ],
         compiler_params=pltpu.CompilerParams(
@@ -669,7 +681,8 @@
     docs = rows * nd * nc
     half = centroids.shape[0] // 2
     held = docs * (2 * features + 4 * half)
-    form = replicated if 2 * held <= VMEM_BYTES else scattered
+    fits = 2 * held <= VMEM_BYTES and nd > 2 and nc > 1 and not nc & (nc - 1)
+    form = replicated if fits else scattered
     return form(nd, nc, embeddings, centroids)
 
 

time: 36.6 us -> 34.7 us (0.948)
  Pallas kernels: 34.5 us -> 32.6 us
    pallas_call x1, Pallas kernels: 34.5 us -> 32.6 us  [replicated(): pl.pallas_call(functools.partial(replicated_kernel, nd, nc), out_shape=(j...]
where the time goes in v3:
time: 34.7 us; the launch traced here: 34.5 us
  Pallas kernels  32.6 us (94%)
  local copies, waits for them, and re-layouts  1.25 us (4%)
  between operations  0.64 us (2%)
    pallas_call x1, Pallas kernels, replicated(): pl.pallas_call(functools.partial(replicated_kernel, nd, nc), out_shape=(j...  32.6 us
    unnamed x2, local copies, waits for them, and re-layouts  1.25 us

profile of v3, /device:TPU:0, one launch (start us, length us, event | category | flops | bytes accessed | tf_op | source)
XLA Modules:
  0.0 34.5 jit_solution(5165522548487447395)
XLA Ops:
  0.6 32.6 %shard_map.41 = (f32[32,1024]{1,0:T(8,128)S(1)}, f32[1,1024]{1,0:T(1,128)S(1)}) custom-call(bf16[128,256]{1,0:T(8,128)(2,1)} %emb_ref.1, bf16[1024,256]{1,0:T(8,128)(2,1)} %cent_ref.1), custom_call_target="tpu_custom_call" | custom-call | tf_op jit(solution)/shard_map/pallas_call | solution.py:641
  33.3 0.7 %copy.6 = f32[32,1024]{1,0:T(8,128)} copy(f32[32,1024]{1,0:T(8,128)S(1)} %get-tuple-element.8) | data formatting | bytes 262144
  33.9 0.6 %copy.7 = f32[1024]{0:T(1024)} copy(f32[1024]{0:T(1024)S(1)} %bitcast.1) | data formatting | bytes 8192

commit v4 on v3

--- a/solution.py
+++ b/solution.py
@@ -417,14 +417,14 @@
         lax.fori_loop(0, half // step, body, 0, unroll=2)
 
     own_copy.wait()
-    cent_copy.wait()
-    scores[mine] = score(mine)
     pl.semaphore_wait(barrier, nb - 1 + nz - 1)
 
     to_plane(mine, 0, far + near)
     to_partner(mine, 0)
     for k in range(1, nz):
         send(own, own, own_ss.at[k], emb_rs.at[mine], (2 * z_peer(k) + core, c))
+    cent_copy.wait()
+    scores[mine] = score(mine)
     column_update([mine], True)
     for k in range(1, nc):
         slot = slot_of(z, core, clu_peer(k))
@@ -548,7 +548,7 @@
     logs = column_receive(0)
     top = functools.reduce(jnp.maximum, logs)
     spread(-log_clusters - (top + jnp.log2(sum(jnp.exp2(x - top) for x in logs))))
-    lax.fori_loop(0, nb, row_first, 0, unroll=4)
+    lax.fori_loop(0, nb, row_first, 0, unroll=8)
     row_send(0, 0)
     for k in range(1, nz):
         across(k, near + far if k == 1 else near)
@@ -564,7 +564,7 @@
             ref = pots.at[z]
             for k in range(1, nz):
                 send(ref, ref, pot_ss.at[k], pot_rs.at[z], (2 * z_peer(k) + core, c))
-        lax.fori_loop(0, half // step, column_next, 0, unroll=4)
+        lax.fori_loop(0, half // step, column_next, 0, unroll=8)
         column_send(it, jnp.sum(jnp.transpose(total[...]), axis=0, keepdims=True))
         if it == 1:
             for k in range(2, nz):
@@ -579,7 +579,7 @@
                 remote(
                     theirs, theirs, pot_ss.at[k], pot_rs.at[z_peer(k)], (partner, c)
                 ).wait_recv()
-            lax.fori_loop(0, nb, functools.partial(row_next, it, k, last), 0, unroll=4)
+            lax.fori_loop(0, nb, functools.partial(row_next, it, k, last), 0, unroll=8)
             row_send(it, k)
         if not last:
             pots[z] = pots[z] - log_docs - jnp.log2(sum(row_receive(it, 0)))
@@ -630,6 +630,11 @@
     mass_ref[:, columns] = pairmass[1]
     for copy in sends:
         copy.wait_send()
+
+
+def store_kernel(part_ref, mass_ref, out_ref, total_ref):
+    out_ref[...] = part_ref[...]
+    total_ref[...] = mass_ref[...].reshape(total_ref.shape)
 
 
 def replicated(nd, nc, embeddings, centroids):
@@ -670,7 +675,16 @@
             collective_id=0, has_side_effects=True, vmem_limit_bytes=VMEM_BYTES
         ),
     )(*(pltpu.with_memory_space_constraint(a, pltpu.HBM) for a in (embeddings, centroids)))
-    return out, mass.reshape(own_cols)
+    return pl.pallas_call(
+        store_kernel,
+        out_shape=(
+            jax.ShapeDtypeStruct((own_f, own_cols), F32),
+            jax.ShapeDtypeStruct((own_cols,), F32),
+        ),
+        in_specs=[pl.BlockSpec(memory_space=pltpu.VMEM)] * 2,
+        out_specs=(pl.BlockSpec(memory_space=pltpu.VMEM),) * 2,
+        compiler_params=pltpu.CompilerParams(vmem_limit_bytes=4 << 20),
+    )(out, mass)
 
 
 VMEM_BYTES = 48 << 20

time: 34.7 us -> 33.9 us (0.977)
  local copies, waits for them, and re-layouts: 1.25 us -> 0 us
  Pallas kernels: 32.6 us -> 33.1 us
    unnamed x2 -> x0, local copies, waits for them, and re-layouts: 1.25 us -> none
    pallas_call x0 -> x1, Pallas kernels: none -> 0.67 us  [replicated(): pl.pallas_call(store_kernel, out_shape=(jax.ShapeDtypeStruct((own_f, own_...]
where the time goes in v4:
time: 33.9 us; the launch traced here: 33.8 us
  Pallas kernels  33.1 us (98%)
  between operations  0.64 us (2%)
    pallas_call x1, Pallas kernels, replicated(): pl.pallas_call(functools.partial(replicated_kernel, nd, nc), out_shape=(j...  32.5 us

profile of v4, /device:TPU:0, one launch (start us, length us, event | category | flops | bytes accessed | tf_op | source)
XLA Modules:
  0.0 33.8 jit_solution(4298008250074742702)
XLA Ops:
  0.6 32.5 %shard_map.41 = (f32[32,1024]{1,0:T(8,128)S(1)}, f32[1,1024]{1,0:T(1,128)S(1)}) custom-call(bf16[128,256]{1,0:T(8,128)(2,1)} %emb_ref.1, bf16[1024,256]{1,0:T(8,128)(2,1)} %cent_ref.1), custom_call_target="tpu_custom_call" | custom-call | tf_op jit(solution)/shard_map/pallas_call | solution.py:646
  33.1 0.7 %shard_map.42 = (f32[32,1024]{1,0:T(8,128)}, f32[1024]{0:T(1024)}) custom-call(f32[32,1024]{1,0:T(8,128)S(1)} %get-tuple-element.4.part_ref, f32[1,1024]{1,0:T(1,128)S(1)} %get-tuple-element.5.mass_ref), custom_call_target="tpu_custom_call" | custom-call | tf_op jit(solution)/shard_map/pallas_call | solution.py:678

commit v5 on v4

--- a/solution.py
+++ b/solution.py
@@ -319,15 +319,21 @@
         bits = [1 << b for b in range(n.bit_length() - 1)]
         return sum(lax.rem(lax.div(i, b) + k // b, 2) * b for b in bits)
 
+    block_peers = [paired(me, k, nb) for k in range(nb)]
+    block_peers = [(p, (2 * z + lax.div(p, nc), lax.rem(p, nc))) for p in block_peers]
+    clu_peers = [paired(c, k, nc) for k in range(nc)]
+    z_peers = [paired(z, k, nz) for k in range(nz)]
+
+    pair_peers = [paired(lax.div(c, 2), k, nc // 2) for k in range(nc // 2)]
+
     def block_peer(k):
-        peer = paired(me, k, nb)
-        return peer, (2 * z + lax.div(peer, nc), lax.rem(peer, nc))
+        return block_peers[k]
 
     def clu_peer(k):
-        return paired(c, k, nc)
+        return clu_peers[k]
 
     def z_peer(k):
-        return paired(z, k, nz)
+        return z_peers[k]
 
     def slot_of(plane, side, cluster):
         return plane * nb + side * nc + cluster
@@ -390,15 +396,17 @@
             centers[...], emb_all[pl.ds(slot, 2)].reshape(2 * rows, features),
             (((1,), (1,)), ((), ())), preferred_element_type=F32,
         ) * (LOG2E / SMOOTHING)
-        scores[slot] = both[:, :rows] + wide[...]
-        scores[slot + 1] = both[:, rows:] + wide[...]
+        for n in range(2):
+            block = both[:, n * rows:(n + 1) * rows]
+            scores[slot + n] = block + wide[...] if k else block
+        return slot, slot + 1
 
     def plane_scores(k, first, count):
         for j in range(2 * first, 2 * (first + count)):
             arrive(slot_of(z_peer(k), other, clu_peer(j)))
         for j in range(first, first + count):
             for side in (core, other):
-                pair_scores(k, side, paired(lax.div(c, 2), j, nc // 2))
+                pair_scores(k, side, pair_peers[j])
 
     def piece(g):
         return pl.ds(pl.multiple_of(g * step, step), step)
@@ -414,7 +422,7 @@
             high[at, :] = new
             return carry
 
-        lax.fori_loop(0, half // step, body, 0, unroll=2)
+        lax.fori_loop(0, half // step, body, 0, unroll=4)
 
     own_copy.wait()
     pl.semaphore_wait(barrier, nb - 1 + nz - 1)
@@ -426,12 +434,17 @@
     cent_copy.wait()
     scores[mine] = score(mine)
     column_update([mine], True)
-    for k in range(1, nc):
-        slot = slot_of(z, core, clu_peer(k))
-        arrive(slot)
-        to_partner(slot, k)
-        scores[slot] = score(slot)
-    column_update([slot_of(z, core, clu_peer(k)) for k in range(1, nc)], False)
+    slot = slot_of(z, core, clu_peer(1))
+    arrive(slot)
+    to_partner(slot, 1)
+    scores[slot] = score(slot)
+    column_update([slot], False)
+    for j in range(1, nc // 2):
+        for k in (2 * j, 2 * j + 1):
+            slot = slot_of(z, core, clu_peer(k))
+            arrive(slot)
+            to_partner(slot, k)
+        column_update(pair_scores(0, core, pair_peers[j]), False)
 
     def from_plane(k):
         slot = slot_of(z_peer(k), core, c)
@@ -447,14 +460,10 @@
 
     if nz > 1:
         from_plane(1)
-    for k in range(nc):
-        slot = slot_of(z, other, clu_peer(k))
-        arrive(slot)
-        scores[slot] = score(slot)
-        if k % 2:
-            column_update([slot_of(z, other, clu_peer(k - 1)), slot], False)
-    if nc % 2:
-        column_update([slot_of(z, other, clu_peer(nc - 1))], False)
+    for j in range(nc // 2):
+        for k in (2 * j, 2 * j + 1):
+            arrive(slot_of(z, other, clu_peer(k)))
+        column_update(pair_scores(0, other, pair_peers[j]), False)
 
     def spread(x):
         wide[...] = jnp.transpose(jnp.broadcast_to(x, (rows, half)))
@@ -490,35 +499,52 @@
     def folded(x, op):
         return functools.reduce(op, [x[8 * i:8 * i + 8] for i in range(tiles)])
 
-    def row_first(b, carry):
-        slot = z * nb + b
-        top = jnp.full((8, rows), -jnp.inf, F32)
-        for g in range(half // step):
-            at = pl.ds(g * step, step)
-            t = scores[slot, at, :] + wide[at, :]
-            scores[slot, at, :] = t
-            top = jnp.maximum(top, folded(t, jnp.maximum))
-        top = jnp.max(top, axis=0, keepdims=True)
-        acc = jnp.zeros((8, rows), F32)
-        for g in range(half // step):
-            at = pl.ds(g * step, step)
-            acc = acc + folded(jnp.exp2(scores[slot, at, :] - top), jnp.add)
-        rowbuf[0, 0, me, pl.ds(b, 1), :] = top + jnp.log2(jnp.sum(acc, axis=0, keepdims=True))
-        return carry
-
-    def row_next(it, k, last, b, carry):
+    def rows_of(parts, op):
+        return jnp.concatenate([op(x, axis=0, keepdims=True) for x in parts], axis=0)
+
+    def row_first():
+        def shift(g, tops):
+            at = piece(g)
+            w = wide[at, :]
+            new = []
+            for b in range(nb):
+                t = scores[z * nb + b, at, :] + w
+                scores[z * nb + b, at, :] = t
+                new.append(jnp.maximum(tops[b], folded(t, jnp.maximum)))
+            return tuple(new)
+
+        def add(g, accs):
+            at = piece(g)
+            return tuple(
+                accs[b] + folded(jnp.exp2(scores[z * nb + b, at, :] - top[b:b + 1]), jnp.add)
+                for b in range(nb)
+            )
+
+        count = half // step
+        low = (jnp.full((8, rows), -jnp.inf, F32),) * nb
+        top = rows_of(lax.fori_loop(0, count, shift, low, unroll=count), jnp.max)
+        zero = (jnp.zeros((8, rows), F32),) * nb
+        total = rows_of(lax.fori_loop(0, count, add, zero, unroll=count), jnp.sum)
+        rowbuf[0, 0, me] = top + jnp.log2(total)
+
+    def row_next(it, k, last):
         plane = z_peer(k)
-        slot = plane * nb + b
-        r = pots[plane, pl.ds(b, 1), :]
-        acc = jnp.zeros((8, rows), F32)
-        for g in range(half // step):
-            at = pl.ds(g * step, step)
-            t = scores[slot, at, :] + wide[at, :]
-            e = jnp.exp2(t + r)
-            scores[slot, at, :] = e if last else t
-            acc = acc + folded(e, jnp.add)
-        rowbuf[it, k, me, pl.ds(b, 1), :] = jnp.sum(acc, axis=0, keepdims=True)
-        return carry
+
+        def body(g, accs):
+            at = piece(g)
+            w = wide[at, :]
+            new = []
+            for b in range(nb):
+                t = scores[plane * nb + b, at, :] + w
+                e = jnp.exp2(t + r[b:b + 1])
+                scores[plane * nb + b, at, :] = e if last else t
+                new.append(accs[b] + folded(e, jnp.add))
+            return tuple(new)
+
+        r = pots[plane]
+        zero = (jnp.zeros((8, rows), F32),) * nb
+        found = lax.fori_loop(0, half // step, body, zero, unroll=half // step)
+        rowbuf[it, k, me] = rows_of(found, jnp.sum)
 
     def column_next(g, carry):
         at = piece(g)
@@ -548,7 +574,7 @@
     logs = column_receive(0)
     top = functools.reduce(jnp.maximum, logs)
     spread(-log_clusters - (top + jnp.log2(sum(jnp.exp2(x - top) for x in logs))))
-    lax.fori_loop(0, nb, row_first, 0, unroll=8)
+    row_first()
     row_send(0, 0)
     for k in range(1, nz):
         across(k, near + far if k == 1 else near)
@@ -561,6 +587,8 @@
     for it in range(1, ITERS):
         last = it == ITERS - 1
         if last:
+            gone = list(sends)
+            sends.clear()
             ref = pots.at[z]
             for k in range(1, nz):
                 send(ref, ref, pot_ss.at[k], pot_rs.at[z], (2 * z_peer(k) + core, c))
@@ -579,11 +607,13 @@
                 remote(
                     theirs, theirs, pot_ss.at[k], pot_rs.at[z_peer(k)], (partner, c)
                 ).wait_recv()
-            lax.fori_loop(0, nb, functools.partial(row_next, it, k, last), 0, unroll=8)
+            row_next(it, k, last)
             row_send(it, k)
         if not last:
             pots[z] = pots[z] - log_docs - jnp.log2(sum(row_receive(it, 0)))
 
+    for copy in gone:
+        copy.wait_send()
     wider = min(half, 256)
 
     def plane_plan(k):
@@ -621,6 +651,8 @@
     columns = pl.ds(pl.multiple_of(core * half, half), half)
     out_ref[:, columns] = features_of(core)[...]
     mass_ref[:, columns] = pairmass[0]
+    for copy in sends:
+        copy.wait_send()
     columns = pl.ds(pl.multiple_of(other * half, half), half)
     remote(pairbuf, pairbuf, pair_ss.at[0], pair_rs.at[0], (partner, c)).wait_recv()
     out_ref[:, columns] = pairbuf[...]
@@ -628,8 +660,6 @@
         pairmass.at[1], pairmass.at[1], pair_ss.at[1], pair_rs.at[1], (partner, c)
     ).wait_recv()
     mass_ref[:, columns] = pairmass[1]
-    for copy in sends:
-        copy.wait_send()
 
 
 def store_kernel(part_ref, mass_ref, out_ref, total_ref):

time: 33.9 us -> 33.1 us (0.976)
  Pallas kernels: 33.1 us -> 32.3 us
    pallas_call x1, Pallas kernels: 32.5 us -> 31.6 us  [replicated(): pl.pallas_call(functools.partial(replicated_kernel, nd, nc), out_shape=(j...]
where the time goes in v5:
time: 33.1 us; the launch traced here: 32.9 us
  Pallas kernels  32.3 us (98%)
  between operations  0.64 us (2%)
    pallas_call x1, Pallas kernels, replicated(): pl.pallas_call(functools.partial(replicated_kernel, nd, nc), out_shape=(j...  31.6 us
    pallas_call x1, Pallas kernels, replicated(): pl.pallas_call(store_kernel, out_shape=(jax.ShapeDtypeStruct((own_f, own_...  0.67 us

profile of v5, /device:TPU:0, one launch (start us, length us, event | category | flops | bytes accessed | tf_op | source)
XLA Modules:
  0.0 32.9 jit_solution(13506174709809581021)
XLA Ops:
  0.6 31.6 %shard_map.41 = (f32[32,1024]{1,0:T(8,128)S(1)}, f32[1,1024]{1,0:T(1,128)S(1)}) custom-call(bf16[128,256]{1,0:T(8,128)(2,1)} %emb_ref.1, bf16[1024,256]{1,0:T(8,128)(2,1)} %cent_ref.1), custom_call_target="tpu_custom_call" | custom-call | tf_op jit(solution)/shard_map/pallas_call | solution.py:676
  32.3 0.7 %shard_map.42 = (f32[32,1024]{1,0:T(8,128)}, f32[1024]{0:T(1024)}) custom-call(f32[32,1024]{1,0:T(8,128)S(1)} %get-tuple-element.4.part_ref, f32[1,1024]{1,0:T(1,128)S(1)} %get-tuple-element.5.mass_ref), custom_call_target="tpu_custom_call" | custom-call | tf_op jit(solution)/shard_map/pallas_call | solution.py:708

commit v6 on v5

--- a/solution.py
+++ b/solution.py
@@ -326,6 +326,8 @@
 
     pair_peers = [paired(lax.div(c, 2), k, nc // 2) for k in range(nc // 2)]
 
+    outward = sorted(range(1, nb), key=lambda k: -(2 * (k % nc).bit_count() + k // nc))
+
     def block_peer(k):
         return block_peers[k]
 
@@ -354,11 +356,9 @@
     mine = slot_of(z, core, c)
     own = emb_all.at[mine]
     own_copy = pltpu.make_async_copy(emb_ref, own, own_sem)
-    own_copy.start()
     cent_copy = pltpu.make_async_copy(
         cent_ref.at[pl.ds(pl.multiple_of(core * half, half), half), :], centers, cent_sem
     )
-    cent_copy.start()
     barrier = pltpu.get_barrier_semaphore()
     for k in range(1, nb):
         pl.semaphore_signal(barrier, inc=1, device_id=block_peer(k)[1], device_id_type=MESH)
@@ -366,6 +366,9 @@
         pl.semaphore_signal(
             barrier, inc=1, device_id=(2 * z_peer(k) + core, c), device_id_type=MESH
         )
+
+    own_copy.start()
+    cent_copy.start()
 
     def score(slot):
         return lax.dot_general(
@@ -422,7 +425,7 @@
             high[at, :] = new
             return carry
 
-        lax.fori_loop(0, half // step, body, 0, unroll=4)
+        lax.fori_loop(0, half // step, body, 0, unroll=8)
 
     own_copy.wait()
     pl.semaphore_wait(barrier, nb - 1 + nz - 1)
@@ -471,7 +474,7 @@
     def column_send(it, x):
         colbuf[it, z] = x
         ref = colbuf.at[it, z]
-        for k in range(1, nz):
+        for k in reversed(range(1, nz)):
             send(ref, ref, col_ss.at[it, k], col_rs.at[it, z], (2 * z_peer(k) + core, c))
 
     def column_receive(it):
@@ -484,7 +487,7 @@
 
     def row_send(it, k):
         ref = rowbuf.at[it, k, me]
-        for j in range(1, nb):
+        for j in outward:
             send(ref, ref, row_ss.at[it, k, j], row_rs.at[it, k, me], block_peer(j)[1])
 
     def row_receive(it, k):
@@ -589,11 +592,12 @@
         if last:
             gone = list(sends)
             sends.clear()
+        lax.fori_loop(0, half // step, column_next, 0, unroll=8)
+        column_send(it, jnp.sum(jnp.transpose(total[...]), axis=0, keepdims=True))
+        if last:
             ref = pots.at[z]
             for k in range(1, nz):
                 send(ref, ref, pot_ss.at[k], pot_rs.at[z], (2 * z_peer(k) + core, c))
-        lax.fori_loop(0, half // step, column_next, 0, unroll=8)
-        column_send(it, jnp.sum(jnp.transpose(total[...]), axis=0, keepdims=True))
         if it == 1:
             for k in range(2, nz):
                 across(k, far)

time: 33.1 us -> 32.6 us (0.985)
  Pallas kernels: 32.3 us -> 31.9 us
    pallas_call x1, Pallas kernels: 31.6 us -> 31.2 us  [replicated(): pl.pallas_call(functools.partial(replicated_kernel, nd, nc), out_shape=(j...]
where the time goes in v6:
time: 32.6 us; the launch traced here: 32.5 us
  Pallas kernels  31.9 us (98%)
  between operations  0.64 us (2%)
    pallas_call x1, Pallas kernels, replicated(): pl.pallas_call(functools.partial(replicated_kernel, nd, nc), out_shape=(j...  31.2 us
    pallas_call x1, Pallas kernels, replicated(): pl.pallas_call(store_kernel, out_shape=(jax.ShapeDtypeStruct((own_f, own_...  0.67 us

profile of v6, /device:TPU:0, one launch (start us, length us, event | category | flops | bytes accessed | tf_op | source)
XLA Modules:
  0.0 32.5 jit_solution(1525063029134249386)
XLA Ops:
  0.6 31.2 %shard_map.41 = (f32[32,1024]{1,0:T(8,128)S(1)}, f32[1,1024]{1,0:T(1,128)S(1)}) custom-call(bf16[128,256]{1,0:T(8,128)(2,1)} %emb_ref.1, bf16[1024,256]{1,0:T(8,128)(2,1)} %cent_ref.1), custom_call_target="tpu_custom_call" | custom-call | tf_op jit(solution)/shard_map/pallas_call | solution.py:680
  31.8 0.7 %shard_map.42 = (f32[32,1024]{1,0:T(8,128)}, f32[1024]{0:T(1024)}) custom-call(f32[32,1024]{1,0:T(8,128)S(1)} %get-tuple-element.4.part_ref, f32[1,1024]{1,0:T(1,128)S(1)} %get-tuple-element.5.mass_ref), custom_call_target="tpu_custom_call" | custom-call | tf_op jit(solution)/shard_map/pallas_call | solution.py:712

commit v7 on v6

--- a/solution.py
+++ b/solution.py
@@ -412,6 +412,8 @@
                 pair_scores(k, side, pair_peers[j])
 
     def piece(g):
+        if isinstance(g, int):
+            return pl.ds(g * step, step)
         return pl.ds(pl.multiple_of(g * step, step), step)
 
     def column_update(slots, first):
@@ -581,8 +583,8 @@
     row_send(0, 0)
     for k in range(1, nz):
         across(k, near + far if k == 1 else near)
-    for k in range(1, nz):
-        plane_scores(k, 0, nc // 2 if k == 1 else 1)
+    if nz > 1:
+        plane_scores(1, 0, nc // 2)
     logs = row_receive(0, 0)
     top = functools.reduce(jnp.maximum, logs)
     pots[z] = -log_docs - (top + jnp.log2(sum(jnp.exp2(x - top) for x in logs)))
@@ -592,7 +594,8 @@
         if last:
             gone = list(sends)
             sends.clear()
-        lax.fori_loop(0, half // step, column_next, 0, unroll=8)
+        for g in range(half // step):
+            column_next(g, 0)
         column_send(it, jnp.sum(jnp.transpose(total[...]), axis=0, keepdims=True))
         if last:
             ref = pots.at[z]
@@ -602,7 +605,7 @@
             for k in range(2, nz):
                 across(k, far)
             for k in range(2, nz):
-                plane_scores(k, 1, nc // 2 - 1)
+                plane_scores(k, 0, nc // 2)
         change = -log_clusters - jnp.log2(sum(column_receive(it)))
         spread(change)
         for k in range(nz if last else 1):

time: 32.6 us -> 32.6 us (level)
  no operation moved by 1% of the time
where the time goes in v7:
time: 32.6 us; the launch traced here: 32.5 us
  Pallas kernels  31.9 us (98%)
  between operations  0.64 us (2%)
    pallas_call x1, Pallas kernels, replicated(): pl.pallas_call(functools.partial(replicated_kernel, nd, nc), out_shape=(j...  31.2 us
    pallas_call x1, Pallas kernels, replicated(): pl.pallas_call(store_kernel, out_shape=(jax.ShapeDtypeStruct((own_f, own_...  0.67 us

profile of v7, /device:TPU:0, one launch (start us, length us, event | category | flops | bytes accessed | tf_op | source)
XLA Modules:
  0.0 32.5 jit_solution(12969419419132292116)
XLA Ops:
  0.6 31.2 %shard_map.41 = (f32[32,1024]{1,0:T(8,128)S(1)}, f32[1,1024]{1,0:T(1,128)S(1)}) custom-call(bf16[128,256]{1,0:T(8,128)(2,1)} %emb_ref.1, bf16[1024,256]{1,0:T(8,128)(2,1)} %cent_ref.1), custom_call_target="tpu_custom_call" | custom-call | tf_op jit(solution)/shard_map/pallas_call | solution.py:683
  31.8 0.7 %shard_map.42 = (f32[32,1024]{1,0:T(8,128)}, f32[1024]{0:T(1024)}) custom-call(f32[32,1024]{1,0:T(8,128)S(1)} %get-tuple-element.4.part_ref, f32[1,1024]{1,0:T(1,128)S(1)} %get-tuple-element.5.mass_ref), custom_call_target="tpu_custom_call" | custom-call | tf_op jit(solution)/shard_map/pallas_call | solution.py:715
